TPU v7x, 32 devices: a whole 2x2x4 slice. The times are simulated.
32 devices in a mesh: groups: 2 (over y), tile: 16 (over z, x, core).
Axes of the slice: x: 2, y: 2, z: 4, core: 2. Of those that a mesh axis runs over, the one named last changes fastest.
Arguments:
- features: bfloat16 [192, 16, 16, 256], P(('groups', 'tile')), parts along dimension 0, may hold values from -6 to 6
- weights: bfloat16 [9, 256, 256], replicated, may hold values from -0.125 to 0.125
- grad_out: bfloat16 [192, 16, 16, 256], P(('groups', 'tile')), parts along dimension 0, may hold values from -6 to 6
- tile_pos: int32 [192], P(('groups', 'tile')), parts along dimension 0, may hold values from -1 to 7, as said below
- neighbours: int32 [192, 8], P(('groups', 'tile')), parts along dimension 0, may hold values from -1 to 15, as said below
Outputs:
- activation: bfloat16 [192, 16, 16, 256], P(('groups', 'tile')), parts along dimension 0
- weight_grad: float32 [18, 256, 256], P('groups'), parts along dimension 0
- input_grad: bfloat16 [192, 16, 16, 256], P(('groups', 'tile')), parts along dimension 0
There are 2 independent parts, one for each index of `groups`. A program takes and returns all parts, laid end to end along the dimension named above; an argument that names none is the same for every part. Nothing has to cross between parts.
Inputs may be any that keep to these rules, and one draw needn't show every extreme that they name: `tile_pos`: each device's 6 slots hold the tissue tiles of its band of 2 x 4 tiles first, in raster order, then empty slots; every device holds 2 or more tissue tiles and at least one device holds 6. A code c names slot c % 6 of the device whose index is the own index plus c // 6 - 1; codes of left and right neighbours name the own device, up and up-diagonal neighbours lie on the own or the preceding device, down and down-diagonal ones on the own or the following device. Neighbours are tissue tiles of the slide's grid and the relation is symmetric; empty slots and missing neighbours have -1.
All inputs are finite; a program needn't handle non-finite values.
Results may differ from a plain program's by a relative error of at most 0.0049.
Values may be sent and summed in bfloat16 or wider, within the bound.
No kernel may reach another device: no remote copies, remote signals or barrier semaphores. Data moves between devices by JAX's collectives and lax.ppermute only.
A program may use at most 64 MiB of HBM per device.

v0:
```python
import math
import jax
import jax.numpy as jnp
from jax import lax
from jax.sharding import PartitionSpec as P

EDGE_PICK = (1, 0, 3, 2, 1, 1, 0, 0)
ROOT_HALF = 0.7071067811865476
INV_ROOT_TAU = 0.3989422804014327


def from_behind(value, axis, steps):
    count = lax.axis_size(axis)
    initial, last = (max(0, -steps), min(count, count - steps))
    return lax.ppermute(value, axis, [(source, source + steps) for source in range(initial, last)])


def gelu_value(preact):
    return preact * (0.5 * (1.0 + lax.erf(preact * ROOT_HALF)))


def gelu_slope(preact):
    cumulative = 0.5 * (1.0 + lax.erf(preact * ROOT_HALF))
    density = jnp.exp(-0.5 * preact * preact) * INV_ROOT_TAU
    return cumulative + preact * density


def edge_rims(field_map):
    return jnp.stack(
        [field_map[:, 0], field_map[:, -1], field_map[:, :, 0], field_map[:, :, -1]], axis=1
    )


def surround(center, gathered):
    upper_row = jnp.concatenate([gathered[:, 4, -1:], gathered[:, 0], gathered[:, 5, :1]], axis=1)
    lower_row = jnp.concatenate([gathered[:, 6, -1:], gathered[:, 1], gathered[:, 7, :1]], axis=1)
    middle = jnp.concatenate(
        [gathered[:, 2][:, :, None], center, gathered[:, 3][:, :, None]], axis=2
    )
    return jnp.concatenate([upper_row[:, None], middle, lower_row[:, None]], axis=1)


def tap_matrix(extended, flipped):
    side_cells = extended.shape[1] - 2
    pieces = []
    for row_tap in range(3):
        for col_tap in range(3):
            row_start = 2 - row_tap if flipped else row_tap
            col_start = 2 - col_tap if flipped else col_tap
            pieces.append(
                extended[:, row_start : row_start + side_cells, col_start : col_start + side_cells]
            )
    stacked = jnp.concatenate(pieces, axis=-1)
    return stacked.reshape(-1, stacked.shape[-1])


def lookup(edge_table, source, linked):
    clipped = jnp.clip(jnp.where(linked, source, 0), 0, edge_table.shape[0] - 1)
    picked = jnp.take(edge_table, clipped.reshape(-1), axis=0).reshape(
        linked.shape + edge_table.shape[1:]
    )
    return jnp.where(linked[:, :, None, None], picked, jnp.zeros((), picked.dtype))


def narrow_sources(neighbours, edge_picks, tile_dev):
    anchor = neighbours // tile_dev
    own_slot = (neighbours - tile_dev) * 4 + edge_picks[None, :]
    return jnp.where(
        anchor == 1,
        own_slot,
        jnp.where(anchor == 0, 4 * tile_dev + neighbours, 3 * tile_dev + neighbours),
    )


def narrow_table(own_rims, upper_rows, lower_rows):
    tile_dev = own_rims.shape[0]
    side_cells = own_rims.shape[2]
    channels = own_rims.shape[3]
    return jnp.concatenate(
        [own_rims.reshape(4 * tile_dev, side_cells, channels), upper_rows, lower_rows], axis=0
    )


def forward_tiles(extended, grad_tiles, tissue_gate, weight_mat):
    tile_count = extended.shape[0]
    side_cells = extended.shape[1] - 2
    channels = weight_mat.shape[1]
    preact = jnp.dot(tap_matrix(extended, False), weight_mat, preferred_element_type=jnp.float32)
    preact = preact.reshape(tile_count, side_cells, side_cells, channels)
    gate_cells = tissue_gate[:, None, None, None]
    act_map = (gelu_value(preact) * gate_cells).astype(jnp.bfloat16)
    slope_map = (grad_tiles.astype(jnp.float32) * gelu_slope(preact) * gate_cells).astype(
        jnp.bfloat16
    )
    return (act_map, slope_map)


def weight_terms(ext_x, slope_map):
    return lax.dot_general(
        tap_matrix(ext_x, False),
        slope_map.reshape(-1, slope_map.shape[-1]),
        (((0,), (0,)), ((), ())),
        preferred_element_type=jnp.float32,
    )


def backward_tiles(ext_g, tissue_gate, flip_mat):
    tile_count = ext_g.shape[0]
    side_cells = ext_g.shape[1] - 2
    channels = flip_mat.shape[1]
    back_map = jnp.dot(tap_matrix(ext_g, True), flip_mat, preferred_element_type=jnp.float32)
    back_map = (
        back_map.reshape(tile_count, side_cells, side_cells, channels)
        * tissue_gate[:, None, None, None]
    )
    return back_map.astype(jnp.bfloat16)


def body(features, weights, grad_out, tile_pos, neighbours):
    tile_dev = features.shape[0]
    side_cells = features.shape[1]
    channels = features.shape[3]
    devices = lax.axis_size("tile")
    tissue = (tile_pos >= 0).astype(jnp.float32)
    weight_mat = weights.reshape(9 * channels, channels)
    flip_mat = jnp.transpose(weights, (0, 2, 1)).reshape(9 * channels, channels)
    edge_picks = jnp.array(EDGE_PICK, dtype=jnp.int32)
    linked = neighbours >= 0
    rims_x = edge_rims(features)
    from_above = from_behind(rims_x[:, 1], "tile", 1)
    from_below = from_behind(rims_x[:, 0], "tile", -1)
    table_x = narrow_table(rims_x, from_above, from_below)
    source = narrow_sources(neighbours, edge_picks, tile_dev)
    ext_x = surround(features, lookup(table_x, source, linked))
    activation, pre_grad = forward_tiles(ext_x, grad_out, tissue, weight_mat)
    rims_g = edge_rims(pre_grad)
    grad_above = from_behind(rims_g[:, 1], "tile", 1)
    grad_below = from_behind(rims_g[:, 0], "tile", -1)
    table_g = narrow_table(rims_g, grad_above, grad_below)
    ext_g = surround(pre_grad, lookup(table_g, source, linked))
    weight_part = weight_terms(ext_x, pre_grad)
    grad_scale = 1.0 / math.sqrt(tile_dev * devices * side_cells * side_cells)
    summed = lax.psum(weight_part, "tile")
    weight_grad = (summed * grad_scale).reshape(9, channels, channels)
    input_grad = backward_tiles(ext_g, tissue, flip_mat)
    return (activation, weight_grad, input_grad)


def solution(mesh):
    in_specs = (
        P(("groups", "tile"), None, None, None),
        P(),
        P(("groups", "tile"), None, None, None),
        P(("groups", "tile")),
        P(("groups", "tile"), None),
    )
    out_specs = (
        P(("groups", "tile"), None, None, None),
        P("groups", None, None),
        P(("groups", "tile"), None, None, None),
    )
    return jax.shard_map(body, mesh=mesh, in_specs=in_specs, out_specs=out_specs, check_vma=False)
```

profile of v0, /device:TPU:0, one launch (start us, length us, event | category | flops | bytes accessed | tf_op | source)
XLA Modules:
  0.0 143.3 jit_solution(6044019779046628402)
XLA Ops:
  7.2 0.0 copy-start.1
  7.2 0.0 all-reduce.2.cloned.1.call-start
  7.2 0.9 slice_bitcast_fusion.11
  8.2 1.3 collective-permute-start.1
  9.5 3.0 %collective-permute-start = (bf16[6,16,256]{2,1,0:T(8,128)(2,1)S(1)}, bf16[6,16,256]{2,1,0:T(8,128)(2,1)S(1)}, u32[]{:S(2)}, u32[]{:S(2)}) collective-permute-start(bf16[6,16,256]{2,1,0:T(8,128)(2,1)S(1)} %get-tuple-element.18), channel_id=1, source_target_pairs={{0,1},{1,2},{2,3},{3,4},{4,5},{5,6},{6,7},{7,8},{8,9},{9,10},{10,1... | collective-permute-start | bytes 147464 | tf_op jit(solution)/shard_map/ppermute | solution.py:15
  12.5 1.3 fusion.14
  13.8 0.7 select_clamp_fusion
  14.5 0.1 reshape.50
  14.6 0.7 broadcast_compare_fusion
  15.3 0.7 compare_convert_fusion
  16.0 0.1 copy.60
  16.1 0.0 copy-done.1
  16.1 1.6 %copy.89 = bf16[9,256,256]{1,2,0:T(8,128)(2,1)} copy(bf16[9,256,256]{2,1,0:T(8,128)(2,1)S(1)} %copy-done.1) | data formatting | bytes 2359296 | tf_op args[1]
  17.7 0.0 copy-start
  17.7 0.0 collective-permute-done.1
  17.7 0.0 collective-permute-done
  17.8 0.6 gather_fusion
  18.3 0.1 broadcast_select_fusion.1
  18.5 0.1 copy_select_fusion.1
  18.7 0.1 copy.70
  18.7 0.1 copy.69
  18.9 0.0 copy-done
  18.9 1.2 pad_maximum_fusion
  20.2 0.1 slice_dynamic-update-slice_fusion.11
  20.2 0.3 slice_dynamic-update-slice_fusion.10
  20.6 0.3 slice_dynamic-update-slice_fusion.9
  20.9 0.4 fusion.10
  21.2 0.1 constant_dynamic-update-slice_fusion
  21.3 0.5 fusion.9
  21.8 0.0 copy-start.3
  21.8 0.1 slice_dynamic-update-slice_fusion.8
  21.9 0.3 slice_dynamic-update-slice_fusion.7
  22.2 0.3 slice_dynamic-update-slice_fusion.6
  22.5 0.4 copy-done.3
  22.9 3.6 %fusion.6 = (bf16[6,16,16,256]{3,2,1,0:T(8,128)(2,1)S(1)}, bf16[6,16,16,256]{3,2,1,0:T(8,128)(2,1)}) fusion(bf16[6,16,16,256]{3,2,1,0:T(8,128)(2,1)S(1)} %copy-done.3, f32[6]{0:T(128)S(1)} %compare_convert_fusion, bf16[6,16,16,2304]{3,2,1,0:T(8,128)(2,1)S(1)} %slice_dynamic-update-slice_fusion.6, bf16[2304,256,1,1]{1,0,3,2:T(8,128)(2,1)S(1)} %bitcast.104), kind=kOutput, calls=%fused_computation.10 | convolution fusion | flops 1817837568 | bytes 10616856 | tf_op jit(solution)/shard_map/dot_general | solution.py:88
  26.5 3.5 %convolution_bitcast_fusion = f32[2304,256]{1,0:T(8,128)} fusion(bf16[6,16,16,2304]{3,2,1,0:T(8,128)(2,1)S(1)} %slice_dynamic-update-slice_fusion.6, bf16[6,16,16,256]{3,2,1,0:T(8,128)(2,1)S(1)} %get-tuple-element.4), kind=kOutput, calls=%fused_computation.2 | convolution fusion | flops 1811939328 | bytes 10223616 | tf_op jit(solution)/shard_map/dot_general | solution.py:99
  30.0 0.2 fusion.13
  30.2 0.0 all-reduce.2.cloned.1.call-update
  30.2 1.3 collective-permute-start.3
  31.5 5.3 %collective-permute-start.2 = (bf16[6,16,256]{2,1,0:T(8,128)(2,1)S(1)}, bf16[6,16,256]{2,1,0:T(8,128)(2,1)S(1)}, u32[]{:S(2)}, u32[]{:S(2)}) collective-permute-start(bf16[6,16,256]{2,1,0:T(8,128)(2,1)S(1)} %get-tuple-element.12), channel_id=1, source_target_pairs={{0,1},{1,2},{2,3},{3,4},{4,5},{5,6},{6,7},{7,8},{8,9},{9,10},{10,1... | collective-permute-start | bytes 147464 | tf_op jit(solution)/shard_map/ppermute | solution.py:15
  36.9 0.0 collective-permute-done.3
  36.9 0.6 collective-permute-done.2
  37.6 0.6 gather_fusion.1
  38.2 0.1 broadcast_select_fusion
  38.3 0.1 copy_select_fusion
  38.5 0.1 copy.80
  38.6 0.1 copy.79
  38.7 1.2 maximum_maximum_fusion.1
  39.9 0.3 slice_dynamic-update-slice_fusion.5
  40.2 0.3 slice_dynamic-update-slice_fusion.4
  40.5 0.1 slice_dynamic-update-slice_fusion.3
  40.6 0.5 fusion.8
  41.1 0.1 constant_dynamic-update-slice_fusion.1
  41.1 0.4 fusion.7
  41.5 0.0 copy-start.2
  41.5 0.3 slice_dynamic-update-slice_fusion.2
  41.8 0.3 slice_dynamic-update-slice_fusion.1
  42.2 0.1 slice_dynamic-update-slice_fusion
  42.2 0.5 copy-done.2
  42.8 3.0 %multiply_convert_fusion = bf16[6,16,16,256]{3,2,1,0:T(8,128)(2,1)} fusion(bf16[6,16,16,2304]{3,2,1,0:T(8,128)(2,1)S(1)} %slice_dynamic-update-slice_fusion, bf16[2304,256,1,1]{1,0,3,2:T(8,128)(2,1)S(1)} %bitcast.105, f32[6]{0:T(128)S(1)} %compare_convert_fusion), kind=kOutput, calls=%fused_computation.11 | convolution fusion | flops 1812725760 | bytes 9043992 | tf_op jit(solution)/shard_map/dot_general | solution.py:111
  45.7 87.5 %all-reduce.2.cloned.1.call-done = f32[2304,256]{1,0:T(8,128)} async-done(((f32[2304,256]{1,0:T(8,128)}), f32[2304,256]{1,0:T(8,128)}) %all-reduce.2.cloned.1.call-update) | async-done | bytes 2359312 | tf_op jit(solution)/shard_map/psum | solution.py:143
  133.2 3.3 %broadcast_multiply_fusion = f32[2304,256]{1,0:T(8,128)} fusion(f32[2304,256]{1,0:T(8,128)} %all-reduce.2.cloned.1.call-done), kind=kLoop, calls=%fused_computation.18 | loop fusion | flops 589824 | bytes 4718592 | tf_op jit(solution)/shard_map/mul | solution.py:144
  (20 shorter events, 0.4 us)
Async XLA Ops:
  7.2 9.0 %copy-start.1 = (bf16[9,256,256]{2,1,0:T(8,128)(2,1)S(1)}, bf16[9,256,256]{2,1,0:T(8,128)(2,1)}, u32[]{:S(2)}) copy-start(bf16[9,256,256]{2,1,0:T(8,128)(2,1)} %param.9) | copy-start | bytes 3538948
  7.2 126.0 %all-reduce.2.cloned.1.call-start = ((), (), s32[]{:S(2)}) async-start(), calls=%async_computation | async-start | bytes 4718592 | tf_op jit(solution)/shard_map/psum | solution.py:143
  8.2 9.6 %collective-permute-start.1 = (bf16[6,16,256]{2,1,0:T(8,128)(2,1)S(1)}, bf16[6,16,256]{2,1,0:T(8,128)(2,1)S(1)}, u32[]{:S(2)}, u32[]{:S(2)}) collective-permute-start(bf16[6,16,256]{2,1,0:T(8,128)(2,1)S(1)} %get-tuple-element.17), channel_id=1, source_target_pairs={{1,0},{2,1},{3,2},{4,3},{5,4},{6,5},{7,6},{8,7},{9,8},{10,9},{11,1... | collective-permute-start | bytes 147464 | tf_op jit(solution)/shard_map/ppermute | solution.py:15
  9.5 8.3 %collective-permute-start = (bf16[6,16,256]{2,1,0:T(8,128)(2,1)S(1)}, bf16[6,16,256]{2,1,0:T(8,128)(2,1)S(1)}, u32[]{:S(2)}, u32[]{:S(2)}) collective-permute-start(bf16[6,16,256]{2,1,0:T(8,128)(2,1)S(1)} %get-tuple-element.18), channel_id=1, source_target_pairs={{0,1},{1,2},{2,3},{3,4},{4,5},{5,6},{6,7},{7,8},{8,9},{9,10},{10,1... | collective-permute-start | bytes 147464 | tf_op jit(solution)/shard_map/ppermute | solution.py:15
  17.7 1.2 copy-start
  21.8 1.1 copy-start.3
  30.2 6.7 %collective-permute-start.3 = (bf16[6,16,256]{2,1,0:T(8,128)(2,1)S(1)}, bf16[6,16,256]{2,1,0:T(8,128)(2,1)S(1)}, u32[]{:S(2)}, u32[]{:S(2)}) collective-permute-start(bf16[6,16,256]{2,1,0:T(8,128)(2,1)S(1)} %get-tuple-element.11), channel_id=1, source_target_pairs={{1,0},{2,1},{3,2},{4,3},{5,4},{6,5},{7,6},{8,7},{9,8},{10,9},{11,1... | collective-permute-start | bytes 147464 | tf_op jit(solution)/shard_map/ppermute | solution.py:15
  31.5 6.0 %collective-permute-start.2 = (bf16[6,16,256]{2,1,0:T(8,128)(2,1)S(1)}, bf16[6,16,256]{2,1,0:T(8,128)(2,1)S(1)}, u32[]{:S(2)}, u32[]{:S(2)}) collective-permute-start(bf16[6,16,256]{2,1,0:T(8,128)(2,1)S(1)} %get-tuple-element.12), channel_id=1, source_target_pairs={{0,1},{1,2},{2,3},{3,4},{4,5},{5,6},{6,7},{7,8},{8,9},{9,10},{10,1... | collective-permute-start | bytes 147464 | tf_op jit(solution)/shard_map/ppermute | solution.py:15
  41.5 1.3 copy-start.2
Sparse Core Ops, SparseCore 0:
  30.4 102.8 all-reduce.1
where the time goes:
time: 144 us; the launch traced here: 143 us
  waiting for transfers between devices  88.1 us (61%)
  between operations  14.4 us (10%)
  starting transfers between devices  11 us (8%)
  other arithmetic  10.2 us (7%)
  matrix products  10 us (7%)
  local copies, waits for them, and re-layouts  9.6 us (7%)
    psum x1, waiting for transfers between devices, body(): summed = lax.psum(weight_part, 'tile')  87.5 us
    ppermute x4, starting transfers between devices, from_behind(): lax.ppermute(value, axis, [(source, source + steps) for source in range(i...  10.9 us
    unnamed x24, local copies, waits for them, and re-layouts  5.97 us
    dot_general x1, matrix products, forward_tiles(): jnp.dot(tap_matrix(extended, False), weight_mat, preferred_element_type=j...  3.56 us
    dot_general x1, matrix products, weight_terms(): lax.dot_general(tap_matrix(ext_x, False), slope_map.reshape(-1, slope_map...  3.52 us
    mul x1, other arithmetic, body(): weight_grad = (summed * grad_scale).reshape(9, channels, channels)  3.27 us
    dot_general x1, matrix products, backward_tiles(): jnp.dot(tap_matrix(ext_g, True), flip_mat, preferred_element_type=jnp.flo...  2.96 us
  transfers between devices with their start and end apart: 5, of which 2 were waited for; matrix products, arithmetic and copies ran while one was open for 9% of the time, Pallas kernels for 0%

commit v1 on v0

--- a/solution.py
+++ b/solution.py
@@ -140,7 +140,7 @@
     ext_g = surround(pre_grad, lookup(table_g, source, linked))
     weight_part = weight_terms(ext_x, pre_grad)
     grad_scale = 1.0 / math.sqrt(tile_dev * devices * side_cells * side_cells)
-    summed = lax.psum(weight_part, "tile")
+    summed = jnp.sum(jax.lax.all_gather(weight_part, "tile"), 0)
     weight_grad = (summed * grad_scale).reshape(9, channels, channels)
     input_grad = backward_tiles(ext_g, tissue, flip_mat)
     return (activation, weight_grad, input_grad)

time: 144 us -> 244 us (1.69)
  waiting for transfers between devices: 88.1 us -> 178 us
  other arithmetic: 10.2 us -> 22 us
    all_gather x0 -> x1, waiting for transfers between devices: none -> 175 us  [body(): summed = jnp.sum(jax.lax.all_gather(weight_part, 'tile'), 0)]
    psum x1 -> x0, waiting for transfers between devices: 87.5 us -> none  [body(): summed = lax.psum(weight_part, 'tile')]
    reduce_sum x0 -> x1, other arithmetic: none -> 13.5 us  [body(): summed = jnp.sum(jax.lax.all_gather(weight_part, 'tile'), 0)]
    ppermute x4, waiting for transfers between devices: 0.61 us -> 3.11 us  [from_behind(): lax.ppermute(value, axis, [(source, source + steps) for source in range(i...]
    unnamed x24 -> x22, local copies, waits for them, and re-layouts: 5.97 us -> 4.86 us
  transfers between devices with their start and end apart: 5 -> 5, of which waited for: 2 -> 3; matrix products, arithmetic and copies ran while one was open for 9% -> 5% of each run, Pallas kernels for 0% -> 0%
where the time goes in v1:
time: 244 us; the launch traced here: 243 us
  waiting for transfers between devices  178 us (73%)
  other arithmetic  22 us (9%)
  between operations  14.4 us (6%)
  starting transfers between devices  10.1 us (4%)
  matrix products  10 us (4%)
  local copies, waits for them, and re-layouts  8.5 us (3%)
    all_gather x1, waiting for transfers between devices, body(): summed = jnp.sum(jax.lax.all_gather(weight_part, 'tile'), 0)  175 us
    reduce_sum x1, other arithmetic, body(): summed = jnp.sum(jax.lax.all_gather(weight_part, 'tile'), 0)  13.5 us
    ppermute x4, starting transfers between devices, from_behind(): lax.ppermute(value, axis, [(source, source + steps) for source in range(i...  10 us
  transfers between devices with their start and end apart: 5, of which 3 were waited for; matrix products, arithmetic and copies ran while one was open for 5% of the time, Pallas kernels for 0%

profile of v1, /device:TPU:0, one launch (start us, length us, event | category | flops | bytes accessed | tf_op | source)
XLA Modules:
  0.0 243.2 jit_solution(13276742248891391736)
XLA Ops:
  7.2 0.0 all-gather.3.cloned.1.call-start
  7.2 0.8 slice_bitcast_fusion.11
  8.1 2.4 collective-permute-start
  10.5 1.3 collective-permute-start.1
  11.8 1.3 fusion.14
  13.1 0.7 select_clamp_fusion
  13.8 0.1 reshape.51
  13.9 0.7 broadcast_compare_fusion
  14.6 0.7 compare_convert_fusion
  15.2 0.0 copy-start
  15.3 0.1 copy.60
  15.4 0.0 collective-permute-done
  15.4 0.3 collective-permute-done.1
  15.7 0.6 gather_fusion
  16.3 0.1 broadcast_select_fusion.1
  16.4 0.1 copy_select_fusion.1
  16.6 0.1 copy.69
  16.7 0.1 copy.70
  16.9 0.0 copy-done
  16.9 1.2 pad_maximum_fusion
  18.1 0.1 slice_dynamic-update-slice_fusion.11
  18.2 0.3 slice_dynamic-update-slice_fusion.10
  18.5 0.3 slice_dynamic-update-slice_fusion.9
  18.8 0.4 fusion.10
  19.2 0.1 constant_dynamic-update-slice_fusion
  19.3 0.5 fusion.9
  19.8 0.0 copy-start.1
  19.8 0.0 copy-start.2
  19.8 0.1 slice_dynamic-update-slice_fusion.8
  19.9 0.3 slice_dynamic-update-slice_fusion.7
  20.2 0.3 slice_dynamic-update-slice_fusion.6
  20.5 0.5 copy-done.1
  21.0 0.2 copy-done.2
  21.2 3.5 %fusion.6 = (bf16[6,16,16,256]{3,2,1,0:T(8,128)(2,1)S(1)}, bf16[6,16,16,256]{3,2,1,0:T(8,128)(2,1)}) fusion(bf16[6,16,16,256]{3,2,1,0:T(8,128)(2,1)S(1)} %copy-done.2, f32[6]{0:T(128)S(1)} %compare_convert_fusion, bf16[6,16,16,2304]{3,2,1,0:T(8,128)(2,1)S(1)} %slice_dynamic-update-slice_fusion.6, bf16[2304,256,1,1]{1,0,3,2:T(8,128)(2,1)S(1)} %bitcast.106), kind=kOutput, calls=%fused_computation.10 | convolution fusion | flops 1817837568 | bytes 10616856 | tf_op jit(solution)/shard_map/dot_general | solution.py:88
  24.8 3.5 %convolution_bitcast_fusion = f32[2304,256]{1,0:T(8,128)} fusion(bf16[6,16,16,2304]{3,2,1,0:T(8,128)(2,1)S(1)} %slice_dynamic-update-slice_fusion.6, bf16[6,16,16,256]{3,2,1,0:T(8,128)(2,1)S(1)} %get-tuple-element.4), kind=kOutput, calls=%fused_computation.2 | convolution fusion | flops 1811939328 | bytes 10223616 | tf_op jit(solution)/shard_map/dot_general | solution.py:99
  28.3 0.0 all-gather.3.cloned.1.call-update
  28.3 0.7 copy.89
  29.1 0.2 fusion.13
  29.3 4.9 %collective-permute-start.2 = (bf16[6,16,256]{2,1,0:T(8,128)(2,1)S(1)}, bf16[6,16,256]{2,1,0:T(8,128)(2,1)S(1)}, u32[]{:S(2)}, u32[]{:S(2)}) collective-permute-start(bf16[6,16,256]{2,1,0:T(8,128)(2,1)S(1)} %get-tuple-element.12), channel_id=1, source_target_pairs={{0,1},{1,2},{2,3},{3,4},{4,5},{5,6},{6,7},{7,8},{8,9},{9,10},{10,1... | collective-permute-start | bytes 147464 | tf_op jit(solution)/shard_map/ppermute | solution.py:15
  34.2 1.5 collective-permute-start.3
  35.7 0.0 collective-permute-done.2
  35.7 2.8 %collective-permute-done.3 = bf16[6,16,256]{2,1,0:T(8,128)(2,1)S(1)} collective-permute-done((bf16[6,16,256]{2,1,0:T(8,128)(2,1)S(1)}, bf16[6,16,256]{2,1,0:T(8,128)(2,1)S(1)}, u32[]{:S(2)}, u32[]{:S(2)}) %collective-permute-start.3) | collective-permute-done | bytes 49184 | tf_op jit(solution)/shard_map/ppermute | solution.py:15
  38.6 0.6 gather_fusion.1
  39.2 0.1 broadcast_select_fusion
  39.3 0.1 copy_select_fusion
  39.5 0.1 copy.79
  39.5 0.1 copy.80
  39.7 1.2 maximum_maximum_fusion.1
  40.9 0.3 slice_dynamic-update-slice_fusion.5
  41.2 0.3 slice_dynamic-update-slice_fusion.4
  41.5 0.1 slice_dynamic-update-slice_fusion.3
  41.6 0.5 fusion.8
  42.1 0.1 constant_dynamic-update-slice_fusion.1
  42.1 0.3 fusion.7
  42.5 0.3 slice_dynamic-update-slice_fusion.2
  42.8 0.3 slice_dynamic-update-slice_fusion.1
  43.1 0.1 slice_dynamic-update-slice_fusion
  43.2 3.0 %multiply_convert_fusion = bf16[6,16,16,256]{3,2,1,0:T(8,128)(2,1)} fusion(bf16[6,16,16,2304]{3,2,1,0:T(8,128)(2,1)S(1)} %slice_dynamic-update-slice_fusion, bf16[2304,256,1,1]{1,0,3,2:T(8,128)(2,1)S(1)} %bitcast.107, f32[6]{0:T(128)S(1)} %compare_convert_fusion), kind=kOutput, calls=%fused_computation.11 | convolution fusion | flops 1812725760 | bytes 9043992 | tf_op jit(solution)/shard_map/dot_general | solution.py:111
  46.2 175.0 %all-gather.3.cloned.1.call-done = f32[36864,256]{1,0:T(8,128)} async-done(((f32[2304,256]{1,0:T(8,128)}), f32[36864,256]{1,0:T(8,128)}) %all-gather.3.cloned.1.call-update) | async-done | bytes 37748752 | tf_op jit(solution)/shard_map/all_gather | solution.py:143
  221.1 13.5 %reduce_sum.9 = f32[2304,256]{1,0:T(8,128)S(1)} reduce(f32[16,2304,256]{2,1,0:T(8,128)} %bitcast.102, f32[]{:T(128)} %constant.24.clone.1), dimensions={0}, to_apply=%region_0.2 | reduce | flops 8847360 | bytes 40108036 | tf_op jit(solution)/shard_map/reduce_sum | solution.py:143
  234.7 1.6 broadcast_multiply_fusion
  (20 shorter events, 0.4 us)
Async XLA Ops:
  7.2 214.0 %all-gather.3.cloned.1.call-start = ((), (), s32[]{:S(2)}) async-start(), calls=%async_computation | async-start | bytes 40108032 | tf_op jit(solution)/shard_map/all_gather | solution.py:143
  8.1 7.4 %collective-permute-start = (bf16[6,16,256]{2,1,0:T(8,128)(2,1)S(1)}, bf16[6,16,256]{2,1,0:T(8,128)(2,1)S(1)}, u32[]{:S(2)}, u32[]{:S(2)}) collective-permute-start(bf16[6,16,256]{2,1,0:T(8,128)(2,1)S(1)} %get-tuple-element.18), channel_id=1, source_target_pairs={{0,1},{1,2},{2,3},{3,4},{4,5},{5,6},{6,7},{7,8},{8,9},{9,10},{10,1... | collective-permute-start | bytes 147464 | tf_op jit(solution)/shard_map/ppermute | solution.py:15
  10.5 5.2 %collective-permute-start.1 = (bf16[6,16,256]{2,1,0:T(8,128)(2,1)S(1)}, bf16[6,16,256]{2,1,0:T(8,128)(2,1)S(1)}, u32[]{:S(2)}, u32[]{:S(2)}) collective-permute-start(bf16[6,16,256]{2,1,0:T(8,128)(2,1)S(1)} %get-tuple-element.17), channel_id=1, source_target_pairs={{1,0},{2,1},{3,2},{4,3},{5,4},{6,5},{7,6},{8,7},{9,8},{10,9},{11,1... | collective-permute-start | bytes 147464 | tf_op jit(solution)/shard_map/ppermute | solution.py:15
  15.2 1.7 copy-start
  19.8 1.3 copy-start.1
  19.8 1.5 copy-start.2
  29.3 6.4 %collective-permute-start.2 = (bf16[6,16,256]{2,1,0:T(8,128)(2,1)S(1)}, bf16[6,16,256]{2,1,0:T(8,128)(2,1)S(1)}, u32[]{:S(2)}, u32[]{:S(2)}) collective-permute-start(bf16[6,16,256]{2,1,0:T(8,128)(2,1)S(1)} %get-tuple-element.12), channel_id=1, source_target_pairs={{0,1},{1,2},{2,3},{3,4},{4,5},{5,6},{6,7},{7,8},{8,9},{9,10},{10,1... | collective-permute-start | bytes 147464 | tf_op jit(solution)/shard_map/ppermute | solution.py:15
  34.2 4.4 %collective-permute-start.3 = (bf16[6,16,256]{2,1,0:T(8,128)(2,1)S(1)}, bf16[6,16,256]{2,1,0:T(8,128)(2,1)S(1)}, u32[]{:S(2)}, u32[]{:S(2)}) collective-permute-start(bf16[6,16,256]{2,1,0:T(8,128)(2,1)S(1)} %get-tuple-element.11), channel_id=1, source_target_pairs={{1,0},{2,1},{3,2},{4,3},{5,4},{6,5},{7,6},{8,7},{9,8},{10,9},{11,1... | collective-permute-start | bytes 147464 | tf_op jit(solution)/shard_map/ppermute | solution.py:15
Sparse Core Ops, SparseCore 0:
  28.5 192.6 all-gather.2
